TPU v7x, 32 devices: a whole 2x2x4 slice. The times are simulated.
32 devices in a mesh: gx: 4 (over y, x), gy: 8 (over z, core).
Axes of the slice: x: 2, y: 2, z: 4, core: 2. Of those that a mesh axis runs over, the one named last changes fastest.
Arguments:
- old_state: float32 [8, 8, 128, 1024], P(None, None, 'gx', 'gy'), may hold values from -6 to 6
- section_prims: float32 [8, 8, 128, 1024], P(None, None, 'gx', 'gy'), may hold values from -3 to 3, as said below
- shear_whole: int32 [1], replicated, may hold values from 0 to 1023
- shear_frac: float32 [1], replicated, may hold values from 0 to 1
Outputs:
- new_state: float32 [8, 8, 128, 1024], P(None, None, 'gx', 'gy')
Inputs may be any that keep to these rules, and one draw needn't show every extreme that they name: section_prims holds density in [0.5, 2] in field 0 and pressure in [0.3, 3] in field 4; the other fields lie in the stated range.
All inputs are finite; a program needn't handle non-finite values.
Results may differ from a plain program's by a relative error of at most 0.0003.
Values sent between devices are 32-bit elements; how exact they have to be, the bound alone decides.
No kernel may reach another device: no remote copies, remote signals or barrier semaphores. Data moves between devices by JAX's collectives and lax.ppermute only.
A program may use at most 128 MiB of HBM per device.

v0:
```python
import jax
import jax.numpy as jnp
from jax import lax
from jax.sharding import PartitionSpec as P

gamma_gas = 5.0 / 3.0
omega_rate = 1.0
shear_rate = 1.5
time_step = 0.1


def with_halo(shard, sides, width):
    for axis, dim in sides:
        size, length = (lax.axis_size(axis), shard.shape[dim])
        up = [(i, (i + 1) % size) for i in range(size)]
        down = [(j, i) for i, j in up]
        last = lax.slice_in_dim(shard, length - width, length, axis=dim)
        first = lax.slice_in_dim(shard, 0, width, axis=dim)
        before = lax.ppermute(last, axis, up)
        after = lax.ppermute(first, axis, down)
        shard = jnp.concatenate([before, shard, after], axis=dim)
    return shard


def conserved(prims):
    rho = prims[0]
    kinetic = 0.5 * rho * (prims[1] * prims[1] + prims[2] * prims[2] + prims[3] * prims[3])
    magnetic = 0.5 * (prims[5] * prims[5] + prims[6] * prims[6] + prims[7] * prims[7])
    energy = prims[4] / (gamma_gas - 1.0) + kinetic + magnetic
    return jnp.stack(
        [rho, rho * prims[1], rho * prims[2], rho * prims[3], energy, prims[5], prims[6], prims[7]]
    )


def fluxes(prims, cons, direction):
    rho = prims[0]
    normal_vel = prims[1 + direction]
    normal_mag = prims[5 + direction]
    ptotal = prims[4] + 0.5 * (prims[5] * prims[5] + prims[6] * prims[6] + prims[7] * prims[7])
    vdotb = prims[1] * prims[5] + prims[2] * prims[6] + prims[3] * prims[7]
    parts = [rho * normal_vel]
    for comp in range(3):
        parts.append(rho * prims[1 + comp] * normal_vel - prims[5 + comp] * normal_mag)
    parts[1 + direction] = parts[1 + direction] + ptotal
    parts.append((cons[4] + ptotal) * normal_vel - normal_mag * vdotb)
    for comp in range(3):
        parts.append(prims[5 + comp] * normal_vel - prims[1 + comp] * normal_mag)
    return jnp.stack(parts)


def fast_speed(prims, direction):
    rho = prims[0]
    sound = gamma_gas * prims[4] / rho
    squares = [prims[5] * prims[5], prims[6] * prims[6], prims[7] * prims[7]]
    alfven = (squares[0] + squares[1] + squares[2]) / rho
    others = [squares[c] for c in range(3) if c != direction]
    transverse = (others[0] + others[1]) / rho
    disc = jnp.square(sound - alfven) + 4.0 * sound * transverse
    return jnp.sqrt(0.5 * (sound + alfven + jnp.sqrt(disc)))


def minmod(first, second):
    return 0.5 * (jnp.sign(first) + jnp.sign(second)) * jnp.minimum(jnp.abs(first), jnp.abs(second))


def rusanov(left, right, direction):
    cons_left = conserved(left)
    cons_right = conserved(right)
    flux_left = fluxes(left, cons_left, direction)
    flux_right = fluxes(right, cons_right, direction)
    speed_left = jnp.abs(left[1 + direction]) + fast_speed(left, direction)
    speed_right = jnp.abs(right[1 + direction]) + fast_speed(right, direction)
    speed = jnp.maximum(speed_left, speed_right)
    return 0.5 * (flux_left + flux_right) - 0.5 * speed * (cons_right - cons_left)


def sweep(padded, axis, direction):
    length = padded.shape[axis]
    cells = length - 4

    def take(arr, start, stop):
        return lax.slice_in_dim(arr, start, stop, axis=axis)

    diff = take(padded, 1, length) - take(padded, 0, length - 1)
    slope = minmod(take(diff, 0, length - 2), take(diff, 1, length - 1))
    left = take(padded, 1, length - 2) + 0.5 * take(slope, 0, length - 3)
    right = take(padded, 2, length - 1) - 0.5 * take(slope, 1, length - 2)
    face = rusanov(left, right, direction)
    return take(face, 1, cells + 1) - take(face, 0, cells)


def sources(core):
    rho = core[0]
    zeros = jnp.zeros_like(rho)
    return jnp.stack(
        [
            zeros,
            2.0 * omega_rate * rho * core[2],
            -(2.0 - shear_rate) * omega_rate * rho * core[1],
            zeros,
            shear_rate * omega_rate * (rho * core[1] * core[2] - core[5] * core[6]),
            zeros,
            -shear_rate * omega_rate * core[5],
            zeros,
        ]
    )


def section_update(radial_rows, azimuthal_rows, old):
    core = azimuthal_rows[:, :, :, 2:-2]
    radial = sweep(radial_rows, 2, 0)
    azimuthal = sweep(azimuthal_rows, 3, 1)
    zpadded = jnp.concatenate([core[:, -2:], core, core[:, :2]], axis=1)
    vertical = sweep(zpadded, 1, 2)
    rates = -(radial + azimuthal + vertical) + sources(core)
    return 0.5 * old + 0.5 * (conserved(core) + time_step * rates)


def on_device(old_state, section_prims, shear_whole, shear_frac):
    padded = with_halo(section_prims, (("gx", 2), ("gy", 3)), 2)
    cells = section_prims.shape[3]
    loop_size = lax.axis_size("gy")
    total = cells * loop_size
    shift_cells = shear_whole[0]
    frac = shear_frac[0]
    back_cells = (total - 1 - shift_cells) % total
    inner_src = padded[:, :, 0:2, 2:-2]
    outer_src = padded[:, :, -2:, 2:-2]
    inner_cycle, outer_cycle = (
        lax.all_gather(inner_src, "gy", axis=3, tiled=True),
        lax.all_gather(outer_src, "gy", axis=3, tiled=True),
    )
    position = lax.axis_index("gy") * cells
    inner_ext = jnp.concatenate([inner_cycle, inner_cycle[..., : cells + 1]], axis=3)
    outer_ext = jnp.concatenate([outer_cycle, outer_cycle[..., : cells + 1]], axis=3)
    inner_win = lax.dynamic_slice_in_dim(inner_ext, (position + shift_cells) % total, cells + 1, 3)
    outer_win = lax.dynamic_slice_in_dim(outer_ext, (position + back_cells) % total, cells + 1, 3)
    inner_ghost = (1.0 - frac) * inner_win[..., :cells] + frac * inner_win[..., 1:]
    outer_ghost = (1.0 - frac) * outer_win[..., 1:] + frac * outer_win[..., :cells]
    radial_index = lax.axis_index("gx")
    left_rows = jnp.where(radial_index == 0, inner_ghost, inner_src)
    right_rows = jnp.where(radial_index == lax.axis_size("gx") - 1, outer_ghost, outer_src)
    azimuthal_rows = padded[:, :, 2:-2, :]
    radial_rows = jnp.concatenate([left_rows, azimuthal_rows[:, :, :, 2:-2], right_rows], axis=2)
    return section_update(radial_rows, azimuthal_rows, old_state)


def solution(mesh):
    in_specs = (P(None, None, "gx", "gy"), P(None, None, "gx", "gy"), P(), P())
    out_specs = P(None, None, "gx", "gy")
    return jax.shard_map(
        on_device, mesh=mesh, in_specs=in_specs, out_specs=out_specs, check_vma=False
    )
```

profile of v0, /device:TPU:0, one launch (start us, length us, event | category | flops | bytes accessed | tf_op | source)
XLA Modules:
  0.0 111.1 jit_solution(10720879476394507808)
XLA Ops:
  0.0 1.9 %copy.188 = f32[8,8,32,128]{3,1,2,0:T(8,128)S(1)} copy(f32[8,8,32,128]{3,2,1,0:T(8,128)} %param.5) | data formatting | bytes 2097152 | tf_op args[1]
  1.9 1.0 copy-done.4
  2.9 0.7 fusion.22
  3.6 3.9 %collective-permute-start.1 = (f32[8,8,2,128]{3,1,2,0:T(8,128)}, f32[8,8,2,128]{3,1,2,0:T(8,128)S(1)}, u32[]{:S(2)}, u32[]{:S(2)}) collective-permute-start(f32[8,8,2,128]{3,1,2,0:T(8,128)} %get-tuple-element.78), channel_id=1, source_target_pairs={{8,0},{16,8},{24,16},{0,24},{9,1},{17,9},{25,17},{1,25},{10,2},{18... | collective-permute-start | bytes 196616 | tf_op jit(solution)/shard_map/ppermute | solution.py:20
  8.4 1.7 %pad_maximum_fusion.5 = (f32[8,9,32,128]{3,2,1,0:T(8,128)}, f32[8,9,32,128]{3,2,1,0:T(8,128)}) fusion(f32[8,8,32,128]{3,2,1,0:T(8,128)S(1)} %copy-done.1, f32[8,2,32,128]{3,2,1,0:T(8,128)S(1)} %get-tuple-element.82, f32[8,2,32,128]{3,2,1,0:T(8,128)S(1)} %get-tuple-element.83), kind=kLoop, calls=%fused_computation.19 | loop fusion | flops 589824 | bytes 3932160 | tf_op jit(solution)/shard_map/concatenate | solution.py:113
  10.1 0.7 constant_dynamic-update-slice_fusion.4
  10.8 0.7 constant_dynamic-update-slice_fusion.65
  12.1 0.4 fusion.20
  12.4 2.1 %copy_subtract_fusion = f32[8,11,32,128]{3,1,2,0:T(8,128)S(1)} fusion(f32[8,11,32,128]{3,2,1,0:T(8,128)S(1)} %get-tuple-element.51, f32[8,11,32,128]{3,2,1,0:T(8,128)S(1)} %get-tuple-element.50), kind=kLoop, calls=%fused_computation.12 | loop fusion | flops 360448 | bytes 4325376 | tf_op jit(solution)/shard_map/sub | solution.py:84
  14.5 1.5 %minimum_multiply_fusion = f32[8,10,32,128]{3,1,2,0:T(8,128)S(1)} fusion(f32[8,11,32,128]{3,1,2,0:T(8,128)S(1)} %copy_subtract_fusion), kind=kLoop, calls=%fused_computation.14 | loop fusion | flops 2621440 | bytes 3932160 | tf_op jit(solution)/shard_map/mul | solution.py:63
  16.1 2.2 %fusion.1 = (f32[8,9,32,128]{3,1,2,0:T(8,128)S(1)}, f32[8,9,32,128]{3,1,2,0:T(8,128)S(1)}) fusion(f32[8,10,32,128]{3,1,2,0:T(8,128)S(1)} %minimum_multiply_fusion, f32[8,9,32,128]{3,2,1,0:T(8,128)S(1)} %copy-done.8, f32[8,9,32,128]{3,2,1,0:T(8,128)S(1)} %copy-done.9), kind=kLoop, calls=%fused_computation.4 | loop fusion | flops 1179648 | bytes 7077888 | tf_op jit(solution)/shard_map/add | solution.py:86
  18.5 1.3 %multiply_bitcast_fusion = (f32[9,32,128]{2,0,1:T(8,128)}, f32[1,9,32,128]{3,1,2,0:T(8,128)S(1)}, f32[1,9,32,128]{3,1,2,0:T(8,128)S(1)}, f32[8,9,32,128]{3,1,2,0:T(8,128)S(1)}) fusion(f32[8,9,32,128]{3,1,2,0:T(8,128)S(1)} %get-tuple-element.49, f32[8,9,32,128]{3,1,2,0:T(8,128)S(1)} %get-tuple-element.48, ...), kind=kLoop, calls=%fused_computation.52 | loop fusion | flops 1622016 | bytes 4341760 | tf_op jit(solution)/shard_map/mul | solution.py:74
  20.5 0.7 subtract_dynamic-update-slice_fusion
  21.3 0.8 constant_dynamic-update-slice_fusion.51
  22.0 0.7 constant_dynamic-update-slice_fusion.50
  22.8 0.7 constant_dynamic-update-slice_fusion.49
  23.6 0.9 subtract_dynamic-update-slice_fusion.9
  24.6 0.8 subtract_dynamic-update-slice_fusion.6
  25.4 0.8 constant_dynamic-update-slice_fusion.56
  26.2 0.7 constant_dynamic-update-slice_fusion.55
  26.9 0.8 constant_dynamic-update-slice_fusion.54
  27.7 0.7 constant_dynamic-update-slice_fusion.64
  28.4 0.8 constant_dynamic-update-slice_fusion.63
  29.1 0.7 constant_dynamic-update-slice_fusion.62
  29.8 0.8 constant_dynamic-update-slice_fusion.61
  30.6 0.7 constant_dynamic-update-slice_fusion.60
  31.2 0.8 constant_dynamic-update-slice_fusion.59
  32.0 0.8 slice_dynamic-update-slice_fusion.6
  32.9 0.7 constant_dynamic-update-slice_fusion.48
  33.6 2.1 %constant_dynamic-update-slice_fusion.53 = f32[8,9,32,128]{3,1,2,0:T(8,128)} fusion(f32[8,9,32,128]{3,1,2,0:T(8,128)} %constant_dynamic-update-slice_fusion.54, f32[1,9,32,128]{3,1,2,0:T(8,128)} %get-tuple-element.25), kind=kLoop, calls=%fused_computation.157 | loop fusion | bytes 524288
  35.7 2.5 %slice_dynamic-update-slice_fusion = (f32[8,9,32,128]{3,1,2,0:T(8,128)}, f32[8,9,32,128]{3,1,2,0:T(8,128)}) fusion(f32[8,9,32,128]{3,1,2,0:T(8,128)} %constant_dynamic-update-slice_fusion.53, f32[8,9,32,128]{3,1,2,0:T(8,128)} %copy-done, f32[8,9,32,128]{3,1,2,0:T(8,128)} %constant_dynamic-update-slice_fusion.48, f32[8,9,32,128]{3,1,2,0:T(8,128)S(1)} %get-tuple-element.49), kind=kLoop, calls=%fused_computation.41 | loop fusion | bytes 2801664 | tf_op jit(solution)/shard_map/stack | solution.py:30
  38.2 4.1 %multiply_subtract_fusion = f32[8,9,32,128]{3,1,2,0:T(8,128)} fusion(f32[8,9,32,128]{3,1,2,0:T(8,128)} %get-tuple-element.89, f32[8,9,32,128]{3,1,2,0:T(8,128)} %get-tuple-element.88, f32[8,9,32,128]{3,1,2,0:T(8,128)S(1)} %copy-done.13, f32[8,9,32,128]{3,1,2,0:T(8,128)S(1)} %copy-done.11, f32[9,32,128]{2,0,1:T(8,128)} %get-tuple-element.19), kind=kLoop, calls=%fused_computation.13 | loop fusion | flops 1474560 | bytes 6045696 | tf_op jit(solution)/shard_map/sub | solution.py:74
  42.3 0.7 constant_dynamic-update-slice_fusion.58
  43.0 15.0 %all_gather.7 = f32[8,8,2,1024]{3,1,2,0:T(8,128)S(1)} all-gather(f32[8,8,2,128]{3,1,2,0:T(8,128)S(1)} %collective-permute-done.1), channel_id=1, replica_groups=mesh['gx'=4,'gy'=8] {'gy'}, dimensions={3}, use_global_device_ids=true | all-gather | bytes 589824 | tf_op jit(solution)/shard_map/all_gather | solution.py:131
  58.1 15.1 %all_gather.6 = f32[8,8,2,1024]{3,1,2,0:T(8,128)S(1)} all-gather(f32[8,8,2,128]{3,1,2,0:T(8,128)S(1)} %collective-permute-done), channel_id=1, replica_groups=mesh['gx'=4,'gy'=8] {'gy'}, dimensions={3}, use_global_device_ids=true | all-gather | bytes 589824 | tf_op jit(solution)/shard_map/all_gather | solution.py:130
  73.4 0.6 constant_dynamic-update-slice_fusion.32
  74.6 0.4 minimum_multiply_fusion.2
  75.2 0.9 multiply_bitcast_fusion.2
  76.2 0.7 constant_dynamic-update-slice_fusion.16
  77.1 1.0 constant_dynamic-update-slice_fusion.8
  78.1 1.0 copy-done.16
  79.1 1.4 %fusion.21 = (f32[8,8,36,2]{3,1,2,0:T(8,128)}, f32[8,8,36,2]{3,1,2,0:T(8,128)S(1)}) fusion(f32[8,8,36,128]{3,1,2,0:T(8,128)S(1)} %get-tuple-element.87), kind=kLoop, calls=%fused_computation.205 | loop fusion | bytes 73728 | tf_op jit(solution)/shard_map/slice | solution.py:17
  80.5 1.8 %copy.194 = f32[8,8,36,2]{2,1,3,0:T(8,128)S(1)} copy(f32[8,8,36,2]{3,1,2,0:T(8,128)} %get-tuple-element.52) | data formatting | bytes 36864 | tf_op jit(solution)/shard_map/slice | solution.py:17
  82.3 0.4 collective-permute-start.2
  82.7 1.2 %copy.196 = f32[8,8,36,2]{2,1,3,0:T(8,128)} copy(f32[8,8,36,2]{3,1,2,0:T(8,128)S(1)} %get-tuple-element.53) | data formatting | bytes 36864 | tf_op jit(solution)/shard_map/slice | solution.py:18
  83.9 3.4 %collective-permute-start.3 = (f32[8,8,36,2]{2,1,3,0:T(8,128)}, f32[8,8,36,2]{2,1,3,0:T(8,128)}, u32[]{:S(2)}, u32[]{:S(2)}) collective-permute-start(f32[8,8,36,2]{2,1,3,0:T(8,128)} %copy.196), channel_id=1, source_target_pairs={{1,0},{2,1},{3,2},{4,3},{5,4},{6,5},{7,6},{0,7},{9,8},{10,9},{11,1... | collective-permute-start | bytes 55304 | tf_op jit(solution)/shard_map/ppermute | solution.py:20
  87.3 0.7 constant_dynamic-update-slice_fusion.15
  88.0 0.7 constant_dynamic-update-slice_fusion.14
  88.8 0.7 constant_dynamic-update-slice_fusion.13
  89.5 0.7 constant_dynamic-update-slice_fusion.21
  90.4 1.1 copy-done.15
  91.8 1.2 %multiply_subtract_fusion.2 = f32[8,8,33,128]{3,1,2,0:T(8,128)} fusion(f32[8,8,33,128]{3,1,2,0:T(8,128)S(1)} %get-tuple-element.93, f32[8,8,33,128]{3,1,2,0:T(8,128)S(1)} %get-tuple-element.92, f32[8,8,33,128]{3,1,2,0:T(8,128)S(1)} %get-tuple-element.60, f32[8,8,33,128]{3,1,2,0:T(8,128)S(1)} %copy-done.19, f32[8,33,128]{2,0,1:T(8,128)S(1)} %get-tuple-element.5), kind=kLoop, calls=%fused_computation.29 | loop fusion | flops 1351680 | bytes 5541888 | tf_op jit(solution)/shard_map/sub | solution.py:74
  92.9 1.5 %copy.195 = f32[8,8,36,2]{3,1,2,0:T(8,128)S(1)} copy(f32[8,8,36,2]{2,1,3,0:T(8,128)} %collective-permute-done.2) | data formatting | bytes 36864 | tf_op jit(solution)/shard_map/ppermute | solution.py:19
  94.5 1.4 %copy.198 = f32[8,8,36,2]{3,1,2,0:T(8,128)S(1)} copy(f32[8,8,36,2]{2,1,3,0:T(8,128)} %collective-permute-done.3) | data formatting | bytes 36864 | tf_op jit(solution)/shard_map/ppermute | solution.py:20
  95.9 1.0 pad_maximum_fusion
  96.9 0.6 slice_subtract_fusion
  97.5 1.4 %minimum_multiply_fusion.1 = f32[8,8,32,130]{3,1,2,0:T(8,128)S(1)} fusion(f32[8,8,32,131]{3,1,2,0:T(8,128)S(1)} %slice_subtract_fusion), kind=kLoop, calls=%fused_computation.16 | loop fusion | flops 2129920 | bytes 3194880 | tf_op jit(solution)/shard_map/mul | solution.py:63
  99.0 1.5 %fusion.3 = (f32[8,8,32,129]{3,1,2,0:T(8,128)S(1)}, f32[8,8,32,129]{3,1,2,0:T(8,128)S(1)}) fusion(f32[8,8,32,130]{3,1,2,0:T(8,128)S(1)} %minimum_multiply_fusion.1, f32[8,8,36,128]{3,1,2,0:T(8,128)S(1)} %copy-done.3, f32[8,8,36,2]{3,1,2,0:T(8,128)S(1)} %copy.195, f32[8,8,36,2]{3,1,2,0:T(8,128)S(1)} %copy.198), kind=kLoop, calls=%fused_computation.9 | loop fusion | flops 1585152 | bytes 5443584 | tf_op jit(solution)/shard_map/add | solution.py:86
  100.6 0.7 multiply_bitcast_fusion.1
  102.9 0.6 multiply_subtract_fusion.1
  103.5 0.6 copy-done.6
  104.1 0.7 copy-done.7
  105.1 4.8 %fusion.12 = f32[8,8,32,128]{3,1,2,0:T(8,128)S(1)} fusion(f32[8,9,32,128]{3,1,2,0:T(8,128)S(1)} %copy-done.7, f32[8,8,32,129]{3,1,2,0:T(8,128)S(1)} %multiply_subtract_fusion.1, f32[8,8,33,128]{3,1,2,0:T(8,128)S(1)} %copy-done.6, f32[8,8,32,128]{3,2,1,0:T(8,128)S(1)} %copy-done.20, f32[8,8,32,128]{3,2,1,0:T(8,128)} %slice_dynamic-update-slice_fusion.6, ...), kind=kLoop, calls=%fused_computation.37 | loop fusion | flops 2883584 | bytes 10485760 | tf_op jit(solution)/shard_map/add | solution.py:116
  109.9 1.2 %copy.207 = f32[8,8,32,128]{3,2,1,0:T(8,128)} copy(f32[8,8,32,128]{3,1,2,0:T(8,128)S(1)} %fusion.12) | data formatting | bytes 2097152 | tf_op jit(solution)/shard_map/add | solution.py:116
  (100 shorter events, 4.8 us)
Async XLA Ops:
  0.0 8.2 %copy-start.1 = (f32[8,8,32,128]{3,2,1,0:T(8,128)S(1)}, f32[8,8,32,128]{3,2,1,0:T(8,128)}, u32[]{:S(2)}) copy-start(f32[8,8,32,128]{3,2,1,0:T(8,128)} %param.5) | copy-start | bytes 3145732
  1.9 1.0 copy-start.4
  3.6 39.4 %collective-permute-start.1 = (f32[8,8,2,128]{3,1,2,0:T(8,128)}, f32[8,8,2,128]{3,1,2,0:T(8,128)S(1)}, u32[]{:S(2)}, u32[]{:S(2)}) collective-permute-start(f32[8,8,2,128]{3,1,2,0:T(8,128)} %get-tuple-element.78), channel_id=1, source_target_pairs={{8,0},{16,8},{24,16},{0,24},{9,1},{17,9},{25,17},{1,25},{10,2},{18... | collective-permute-start | bytes 196616 | tf_op jit(solution)/shard_map/ppermute | solution.py:20
  7.5 50.6 %collective-permute-start = (f32[8,8,2,128]{3,1,2,0:T(8,128)}, f32[8,8,2,128]{3,1,2,0:T(8,128)S(1)}, u32[]{:S(2)}, u32[]{:S(2)}) collective-permute-start(f32[8,8,2,128]{3,1,2,0:T(8,128)} %get-tuple-element.79), channel_id=1, source_target_pairs={{0,8},{8,16},{16,24},{24,0},{1,9},{9,17},{17,25},{25,1},{2,10},{10... | collective-permute-start | bytes 196616 | tf_op jit(solution)/shard_map/ppermute | solution.py:19
  14.5 1.5 %copy-start.8 = (f32[8,9,32,128]{3,2,1,0:T(8,128)S(1)}, f32[8,9,32,128]{3,2,1,0:T(8,128)}, u32[]{:S(2)}) copy-start(f32[8,9,32,128]{3,2,1,0:T(8,128)} %get-tuple-element.80) | copy-start | bytes 3538948
  14.5 1.6 %copy-start.9 = (f32[8,9,32,128]{3,2,1,0:T(8,128)S(1)}, f32[8,9,32,128]{3,2,1,0:T(8,128)}, u32[]{:S(2)}) copy-start(f32[8,9,32,128]{3,2,1,0:T(8,128)} %get-tuple-element.81) | copy-start | bytes 3538948
  18.3 8.5 %copy-start = (f32[8,9,32,128]{3,1,2,0:T(8,128)}, f32[8,9,32,128]{3,1,2,0:T(8,128)S(1)}, u32[]{:S(2)}) copy-start(f32[8,9,32,128]{3,1,2,0:T(8,128)S(1)} %get-tuple-element.48) | copy-start | bytes 3538948
  21.3 3.2 %copy-start.10 = (f32[8,9,32,128]{3,1,2,0:T(8,128)}, f32[8,9,32,128]{3,1,2,0:T(8,128)S(1)}, u32[]{:S(2)}) copy-start(f32[8,9,32,128]{3,1,2,0:T(8,128)S(1)} %get-tuple-element.43) | copy-start | bytes 3538948
  25.4 5.2 %copy-start.12 = (f32[8,9,32,128]{3,1,2,0:T(8,128)}, f32[8,9,32,128]{3,1,2,0:T(8,128)S(1)}, u32[]{:S(2)}) copy-start(f32[8,9,32,128]{3,1,2,0:T(8,128)S(1)} %get-tuple-element.45) | copy-start | bytes 3538948
  32.9 5.4 %copy-start.11 = (f32[8,9,32,128]{3,1,2,0:T(8,128)S(1)}, f32[8,9,32,128]{3,1,2,0:T(8,128)}, u32[]{:S(2)}) copy-start(f32[8,9,32,128]{3,1,2,0:T(8,128)} %copy-done.10) | copy-start | bytes 3538948
  32.9 5.4 %copy-start.13 = (f32[8,9,32,128]{3,1,2,0:T(8,128)S(1)}, f32[8,9,32,128]{3,1,2,0:T(8,128)}, u32[]{:S(2)}) copy-start(f32[8,9,32,128]{3,1,2,0:T(8,128)} %copy-done.12) | copy-start | bytes 3538948
  73.2 1.2 %copy-start.5 = (f32[8,8,32,128]{3,1,2,0:T(8,128)S(1)}, f32[8,8,32,128]{3,1,2,0:T(8,128)}, u32[]{:S(2)}) copy-start(f32[8,8,32,128]{3,1,2,0:T(8,128)} %copy-done.4) | copy-start | bytes 3145732
  74.3 4.8 %copy-start.2 = (f32[8,8,36,128]{3,1,2,0:T(8,128)}, f32[8,8,36,128]{3,1,2,0:T(8,128)S(1)}, u32[]{:S(2)}) copy-start(f32[8,8,36,128]{3,1,2,0:T(8,128)S(1)} %get-tuple-element.87) | copy-start | bytes 3538948
  76.9 1.2 %copy-start.18 = (f32[8,8,33,128]{3,1,2,0:T(8,128)}, f32[8,8,33,128]{3,1,2,0:T(8,128)S(1)}, u32[]{:S(2)}) copy-start(f32[8,8,33,128]{3,1,2,0:T(8,128)S(1)} %get-tuple-element.8) | copy-start | bytes 3244036
  78.1 1.0 copy-start.16
  82.3 10.7 %collective-permute-start.2 = (f32[8,8,36,2]{2,1,3,0:T(8,128)S(1)}, f32[8,8,36,2]{2,1,3,0:T(8,128)}, u32[]{:S(2)}, u32[]{:S(2)}) collective-permute-start(f32[8,8,36,2]{2,1,3,0:T(8,128)S(1)} %copy.194), channel_id=1, source_target_pairs={{0,1},{1,2},{2,3},{3,4},{4,5},{5,6},{6,7},{7,0},{8,9},{9,10},{10,1... | collective-permute-start | bytes 55304 | tf_op jit(solution)/shard_map/ppermute | solution.py:19
  83.9 5.6 %copy-start.22 = (f32[1,8,33,128]{3,1,2,0:T(8,128)S(1)}, f32[1,8,33,128]{3,1,2,0:T(8,128)}, u32[]{:S(2)}) copy-start(f32[1,8,33,128]{3,1,2,0:T(8,128)} %get-tuple-element.9) | copy-start | bytes 405508
  83.9 6.3 %copy-start.14 = (f32[8,8,33,128]{3,1,2,0:T(8,128)S(1)}, f32[8,8,33,128]{3,1,2,0:T(8,128)}, u32[]{:S(2)}) copy-start(f32[8,8,33,128]{3,1,2,0:T(8,128)} %get-tuple-element.66) | copy-start | bytes 3244036
  83.9 6.3 %copy-start.17 = (f32[8,8,33,128]{3,1,2,0:T(8,128)S(1)}, f32[8,8,33,128]{3,1,2,0:T(8,128)}, u32[]{:S(2)}) copy-start(f32[8,8,33,128]{3,1,2,0:T(8,128)} %copy-done.16) | copy-start | bytes 3244036
  83.9 10.6 %collective-permute-start.3 = (f32[8,8,36,2]{2,1,3,0:T(8,128)}, f32[8,8,36,2]{2,1,3,0:T(8,128)}, u32[]{:S(2)}, u32[]{:S(2)}) collective-permute-start(f32[8,8,36,2]{2,1,3,0:T(8,128)} %copy.196), channel_id=1, source_target_pairs={{1,0},{2,1},{3,2},{4,3},{5,4},{6,5},{7,6},{0,7},{9,8},{10,9},{11,1... | collective-permute-start | bytes 55304 | tf_op jit(solution)/shard_map/ppermute | solution.py:20
  88.8 1.6 %copy-start.21 = (f32[1,8,33,128]{3,1,2,0:T(8,128)S(1)}, f32[1,8,33,128]{3,1,2,0:T(8,128)}, u32[]{:S(2)}) copy-start(f32[1,8,33,128]{3,1,2,0:T(8,128)} %get-tuple-element.11) | copy-start | bytes 405508
  90.2 1.2 %copy-start.15 = (f32[8,8,33,128]{3,1,2,0:T(8,128)S(1)}, f32[8,8,33,128]{3,1,2,0:T(8,128)}, u32[]{:S(2)}) copy-start(f32[8,8,33,128]{3,1,2,0:T(8,128)} %constant_dynamic-update-slice_fusion.21) | copy-start | bytes 3244036
  90.2 1.6 %copy-start.19 = (f32[8,8,33,128]{3,1,2,0:T(8,128)S(1)}, f32[8,8,33,128]{3,1,2,0:T(8,128)}, u32[]{:S(2)}) copy-start(f32[8,8,33,128]{3,1,2,0:T(8,128)} %get-tuple-element.54) | copy-start | bytes 3244036
  92.9 2.9 %copy-start.3 = (f32[8,8,36,128]{3,1,2,0:T(8,128)S(1)}, f32[8,8,36,128]{3,1,2,0:T(8,128)}, u32[]{:S(2)}) copy-start(f32[8,8,36,128]{3,1,2,0:T(8,128)} %copy-done.2) | copy-start | bytes 3538948
  102.9 1.2 %copy-start.6 = (f32[8,8,33,128]{3,1,2,0:T(8,128)S(1)}, f32[8,8,33,128]{3,1,2,0:T(8,128)}, u32[]{:S(2)}) copy-start(f32[8,8,33,128]{3,1,2,0:T(8,128)} %multiply_subtract_fusion.2) | copy-start | bytes 3244036
  102.9 1.9 %copy-start.7 = (f32[8,9,32,128]{3,1,2,0:T(8,128)S(1)}, f32[8,9,32,128]{3,1,2,0:T(8,128)}, u32[]{:S(2)}) copy-start(f32[8,9,32,128]{3,1,2,0:T(8,128)} %multiply_subtract_fusion) | copy-start | bytes 3538948
  102.9 2.2 %copy-start.20 = (f32[8,8,32,128]{3,2,1,0:T(8,128)S(1)}, f32[8,8,32,128]{3,2,1,0:T(8,128)}, u32[]{:S(2)}) copy-start(f32[8,8,32,128]{3,2,1,0:T(8,128)} %param.4) | copy-start | bytes 3145732
where the time goes:
time: 112 us; the launch traced here: 111 us
  other arithmetic  43.6 us (39%)
  blocking collectives  30.1 us (27%)
  local copies, waits for them, and re-layouts  27.7 us (25%)
  starting transfers between devices  7.7 us (7%)
  between operations  1.96 us (2%)
    all_gather x1, blocking collectives, on_device(): lax.all_gather(inner_src, 'gy', axis=3, tiled=True)  15.1 us
    all_gather x1, blocking collectives, on_device(): lax.all_gather(outer_src, 'gy', axis=3, tiled=True)  15 us
    unnamed x50, other arithmetic  14.1 us
    unnamed x58, local copies, waits for them, and re-layouts  14 us
    ppermute x2, starting transfers between devices, with_halo(): after = lax.ppermute(first, axis, down)  7.32 us
    sub x3, other arithmetic, rusanov(): 0.5 * (flux_left + flux_right) - 0.5 * speed * (cons_right - cons_left)  5.88 us
    add x1, other arithmetic, section_update(): return 0.5 * old + 0.5 * (conserved(core) + time_step * rates)  4.85 us
    add x3, other arithmetic, sweep(): left = take(padded, 1, length - 2) + 0.5 * take(slope, 0, length - 3)  3.84 us
  transfers between devices with their start and end apart: 4, of which 0 were waited for; matrix products, arithmetic and copies ran while one was open for 37% of the time, Pallas kernels for 0%

commit v1 on v0

--- a/solution.py
+++ b/solution.py
@@ -7,6 +7,28 @@
 omega_rate = 1.0
 shear_rate = 1.5
 time_step = 0.1
+
+
+def joined_along(blocks, dim):
+    dims = list(blocks.shape[1:])
+    dims[dim] *= blocks.shape[0]
+    return jnp.moveaxis(blocks, 0, dim).reshape(dims)
+
+
+def collect(x, axis, dim):
+    length = lax.axis_size(axis)
+    pairs = [(i, (i + 1) % length) for i in range(length)]
+    back = [(b, a) for a, b in pairs]
+    lower, upper = ([], [])
+    for turn in range(length - 1):
+        if turn % 2 == 0:
+            lower.append(lax.ppermute(lower[-1] if lower else x, axis, pairs))
+        else:
+            upper.append(lax.ppermute(upper[-1] if upper else x, axis, back))
+    parts = jnp.stack([*lower[::-1], x, *upper])
+    shift = lax.axis_index(axis) - len(lower)
+    parts = parts[(jnp.arange(length) - shift) % length]
+    return joined_along(parts, dim)
 
 
 def with_halo(shard, sides, width):
@@ -127,7 +149,7 @@
     inner_src = padded[:, :, 0:2, 2:-2]
     outer_src = padded[:, :, -2:, 2:-2]
     inner_cycle, outer_cycle = (
-        lax.all_gather(inner_src, "gy", axis=3, tiled=True),
+        collect(inner_src, "gy", 3),
         lax.all_gather(outer_src, "gy", axis=3, tiled=True),
     )
     position = lax.axis_index("gy") * cells

time: 112 us -> 116 us (1.036)
  blocking collectives: 30.1 us -> 15 us
  waiting for transfers between devices: 0.01 us -> 11.1 us
  starting transfers between devices: 7.7 us -> 15.2 us
    all_gather x1 -> x0, blocking collectives: 15.1 us -> none  [on_device(): lax.all_gather(inner_src, 'gy', axis=3, tiled=True)]
    ppermute x0 -> x7, waiting for transfers between devices: none -> 11.1 us  [the longest x4 7.54 us: collect(): lower.append(lax.ppermute(lower[-1] if lower else x, axis, pairs))]
    ppermute x0 -> x7, starting transfers between devices: none -> 7.72 us  [the longest x3 7.71 us: collect(): upper.append(lax.ppermute(upper[-1] if upper else x, axis, back))]
    ppermute x2, starting transfers between devices: 7.32 us -> 4.54 us  [with_halo(): after = lax.ppermute(first, axis, down)]
    ppermute x2, starting transfers between devices: 0.39 us -> 2.98 us  [with_halo(): before = lax.ppermute(last, axis, up)]
    unnamed x58 -> x65, local copies, waits for them, and re-layouts: 14 us -> 14.1 us
  transfers between devices with their start and end apart: 4 -> 11, of which waited for: 0 -> 4; matrix products, arithmetic and copies ran while one was open for 37% -> 36% of each run, Pallas kernels for 0% -> 0%
where the time goes in v1:
time: 116 us; the launch traced here: 115 us
  other arithmetic  43.6 us (38%)
  local copies, waits for them, and re-layouts  28.4 us (24%)
  starting transfers between devices  15.2 us (13%)
  blocking collectives  15 us (13%)
  waiting for transfers between devices  11.1 us (10%)
  between operations  2.03 us (2%)
    all_gather x1, blocking collectives, on_device(): lax.all_gather(outer_src, 'gy', axis=3, tiled=True)  15 us
    unnamed x50, other arithmetic  14.2 us
    unnamed x65, local copies, waits for them, and re-layouts  14.1 us
    ppermute x3, starting transfers between devices, collect(): upper.append(lax.ppermute(upper[-1] if upper else x, axis, back))  7.71 us
    ppermute x4, waiting for transfers between devices, collect(): lower.append(lax.ppermute(lower[-1] if lower else x, axis, pairs))  7.54 us
    sub x3, other arithmetic, rusanov(): 0.5 * (flux_left + flux_right) - 0.5 * speed * (cons_right - cons_left)  5.87 us
    add x1, other arithmetic, section_update(): return 0.5 * old + 0.5 * (conserved(core) + time_step * rates)  4.85 us
    ppermute x2, starting transfers between devices, with_halo(): after = lax.ppermute(first, axis, down)  4.54 us
  transfers between devices with their start and end apart: 11, of which 4 were waited for; matrix products, arithmetic and copies ran while one was open for 36% of the time, Pallas kernels for 0%

profile of v1, /device:TPU:0, one launch (start us, length us, event | category | flops | bytes accessed | tf_op | source)
XLA Modules:
  0.0 115.5 jit_solution(14060652616097353167)
XLA Ops:
  0.0 1.9 %copy.201 = f32[8,8,32,128]{3,1,2,0:T(8,128)S(1)} copy(f32[8,8,32,128]{3,2,1,0:T(8,128)} %param.5) | data formatting | bytes 2097152 | tf_op args[1]
  1.9 1.0 copy-done.4
  2.9 0.7 fusion.24
  3.6 2.9 %collective-permute-start = (f32[8,8,2,128]{3,1,2,0:T(8,128)}, f32[8,8,2,128]{3,1,2,0:T(8,128)S(1)}, u32[]{:S(2)}, u32[]{:S(2)}) collective-permute-start(f32[8,8,2,128]{3,1,2,0:T(8,128)} %get-tuple-element.79), channel_id=1, source_target_pairs={{0,8},{8,16},{16,24},{24,0},{1,9},{9,17},{17,25},{25,1},{2,10},{10... | collective-permute-start | bytes 196616 | tf_op jit(solution)/shard_map/ppermute | solution.py:41
  6.5 1.0 collective-permute-start.8
  8.3 1.7 %pad_maximum_fusion.5 = (f32[8,9,32,128]{3,2,1,0:T(8,128)}, f32[8,9,32,128]{3,2,1,0:T(8,128)}) fusion(f32[8,8,32,128]{3,2,1,0:T(8,128)S(1)} %copy-done.1, f32[8,2,32,128]{3,2,1,0:T(8,128)S(1)} %get-tuple-element.82, f32[8,2,32,128]{3,2,1,0:T(8,128)S(1)} %get-tuple-element.83), kind=kLoop, calls=%fused_computation.20 | loop fusion | flops 589824 | bytes 3932160 | tf_op jit(solution)/shard_map/concatenate | solution.py:135
  10.1 0.7 constant_dynamic-update-slice_fusion.4
  10.7 0.7 constant_dynamic-update-slice_fusion.73
  12.4 2.1 %copy_subtract_fusion = f32[8,11,32,128]{3,1,2,0:T(8,128)S(1)} fusion(f32[8,11,32,128]{3,2,1,0:T(8,128)S(1)} %get-tuple-element.51, f32[8,11,32,128]{3,2,1,0:T(8,128)S(1)} %get-tuple-element.50), kind=kLoop, calls=%fused_computation.13 | loop fusion | flops 360448 | bytes 4325376 | tf_op jit(solution)/shard_map/sub | solution.py:106
  14.5 1.5 %minimum_multiply_fusion = f32[8,10,32,128]{3,1,2,0:T(8,128)S(1)} fusion(f32[8,11,32,128]{3,1,2,0:T(8,128)S(1)} %copy_subtract_fusion), kind=kLoop, calls=%fused_computation.15 | loop fusion | flops 2621440 | bytes 3932160 | tf_op jit(solution)/shard_map/mul | solution.py:85
  16.1 2.2 %fusion.1 = (f32[8,9,32,128]{3,1,2,0:T(8,128)S(1)}, f32[8,9,32,128]{3,1,2,0:T(8,128)S(1)}) fusion(f32[8,10,32,128]{3,1,2,0:T(8,128)S(1)} %minimum_multiply_fusion, f32[8,9,32,128]{3,2,1,0:T(8,128)S(1)} %copy-done.8, f32[8,9,32,128]{3,2,1,0:T(8,128)S(1)} %copy-done.9), kind=kLoop, calls=%fused_computation.5 | loop fusion | flops 1179648 | bytes 7077888 | tf_op jit(solution)/shard_map/add | solution.py:108
  18.5 1.4 %multiply_bitcast_fusion = (f32[9,32,128]{2,0,1:T(8,128)}, f32[1,9,32,128]{3,1,2,0:T(8,128)S(1)}, f32[1,9,32,128]{3,1,2,0:T(8,128)S(1)}, f32[8,9,32,128]{3,1,2,0:T(8,128)S(1)}) fusion(f32[8,9,32,128]{3,1,2,0:T(8,128)S(1)} %get-tuple-element.49, f32[8,9,32,128]{3,1,2,0:T(8,128)S(1)} %get-tuple-element.48, ...), kind=kLoop, calls=%fused_computation.54 | loop fusion | flops 1622016 | bytes 4341760 | tf_op jit(solution)/shard_map/mul | solution.py:96
  20.5 0.7 subtract_dynamic-update-slice_fusion
  21.2 0.8 constant_dynamic-update-slice_fusion.59
  22.0 0.7 constant_dynamic-update-slice_fusion.58
  22.8 0.7 constant_dynamic-update-slice_fusion.57
  23.6 0.9 subtract_dynamic-update-slice_fusion.9
  24.6 0.7 subtract_dynamic-update-slice_fusion.6
  25.4 0.8 constant_dynamic-update-slice_fusion.64
  26.2 0.7 constant_dynamic-update-slice_fusion.63
  26.9 0.8 constant_dynamic-update-slice_fusion.62
  27.7 0.7 constant_dynamic-update-slice_fusion.72
  28.4 0.7 constant_dynamic-update-slice_fusion.71
  29.1 0.7 constant_dynamic-update-slice_fusion.70
  29.8 0.8 constant_dynamic-update-slice_fusion.69
  30.6 0.7 constant_dynamic-update-slice_fusion.68
  31.2 0.8 constant_dynamic-update-slice_fusion.67
  32.0 0.8 slice_dynamic-update-slice_fusion.6
  32.8 0.7 constant_dynamic-update-slice_fusion.56
  33.5 2.2 %constant_dynamic-update-slice_fusion.61 = f32[8,9,32,128]{3,1,2,0:T(8,128)} fusion(f32[8,9,32,128]{3,1,2,0:T(8,128)} %constant_dynamic-update-slice_fusion.62, f32[1,9,32,128]{3,1,2,0:T(8,128)} %get-tuple-element.25), kind=kLoop, calls=%fused_computation.159 | loop fusion | bytes 524288
  35.7 2.5 %slice_dynamic-update-slice_fusion = (f32[8,9,32,128]{3,1,2,0:T(8,128)}, f32[8,9,32,128]{3,1,2,0:T(8,128)}) fusion(f32[8,9,32,128]{3,1,2,0:T(8,128)} %constant_dynamic-update-slice_fusion.61, f32[8,9,32,128]{3,1,2,0:T(8,128)} %copy-done, f32[8,9,32,128]{3,1,2,0:T(8,128)} %constant_dynamic-update-slice_fusion.56, f32[8,9,32,128]{3,1,2,0:T(8,128)S(1)} %get-tuple-element.49), kind=kLoop, calls=%fused_computation.42 | loop fusion | bytes 2801664 | tf_op jit(solution)/shard_map/stack | solution.py:52
  38.2 4.1 %multiply_subtract_fusion = f32[8,9,32,128]{3,1,2,0:T(8,128)} fusion(f32[8,9,32,128]{3,1,2,0:T(8,128)} %get-tuple-element.89, f32[8,9,32,128]{3,1,2,0:T(8,128)} %get-tuple-element.88, f32[8,9,32,128]{3,1,2,0:T(8,128)S(1)} %copy-done.13, f32[8,9,32,128]{3,1,2,0:T(8,128)S(1)} %copy-done.11, f32[9,32,128]{2,0,1:T(8,128)} %get-tuple-element.19), kind=kLoop, calls=%fused_computation.14 | loop fusion | flops 1474560 | bytes 6045696 | tf_op jit(solution)/shard_map/sub | solution.py:96
  42.3 0.7 constant_dynamic-update-slice_fusion.66
  43.0 5.5 %collective-permute-done.1 = f32[8,8,2,128]{3,1,2,0:T(8,128)S(1)} collective-permute-done((f32[8,8,2,128]{3,1,2,0:T(8,128)S(1)}, f32[8,8,2,128]{3,1,2,0:T(8,128)S(1)}, u32[]{:S(2)}, u32[]{:S(2)}) %collective-permute-start.1) | collective-permute-done | bytes 65568 | tf_op jit(solution)/shard_map/ppermute | solution.py:25
  48.4 3.5 %collective-permute-start.5 = (f32[8,8,2,128]{3,1,2,0:T(8,128)S(1)}, f32[8,8,2,128]{3,1,2,0:T(8,128)S(1)}, u32[]{:S(2)}, u32[]{:S(2)}) collective-permute-start(f32[8,8,2,128]{3,1,2,0:T(8,128)S(1)} %collective-permute-done), channel_id=1, source_target_pairs={{1,0},{2,1},{3,2},{4,3},{5,4},{6,5},{7,6},{0,7},{9,8},{10,9},{11,1... | collective-permute-start | bytes 196616 | tf_op jit(solution)/shard_map/ppermute | solution.py:27
  52.0 2.0 %collective-permute-done.2 = f32[8,8,2,128]{3,1,2,0:T(8,128)S(1)} collective-permute-done((f32[8,8,2,128]{3,1,2,0:T(8,128)S(1)}, f32[8,8,2,128]{3,1,2,0:T(8,128)S(1)}, u32[]{:S(2)}, u32[]{:S(2)}) %collective-permute-start.2) | collective-permute-done | bytes 65568 | tf_op jit(solution)/shard_map/ppermute | solution.py:25
  54.0 15.0 %all_gather.3 = f32[8,8,2,1024]{3,1,2,0:T(8,128)S(1)} all-gather(f32[8,8,2,128]{3,1,2,0:T(8,128)S(1)} %collective-permute-done.8), channel_id=1, replica_groups=mesh['gx'=4,'gy'=8] {'gy'}, dimensions={3}, use_global_device_ids=true | all-gather | bytes 589824 | tf_op jit(solution)/shard_map/all_gather | solution.py:153
  69.8 1.7 %collective-permute-done.6 = f32[8,8,2,128]{3,1,2,0:T(8,128)S(1)} collective-permute-done((f32[8,8,2,128]{3,1,2,0:T(8,128)S(1)}, f32[8,8,2,128]{3,1,2,0:T(8,128)S(1)}, u32[]{:S(2)}, u32[]{:S(2)}) %collective-permute-start.6) | collective-permute-done | bytes 65568 | tf_op jit(solution)/shard_map/ppermute | solution.py:27
  71.6 3.6 %collective-permute-start.7 = (f32[8,8,2,128]{3,1,2,0:T(8,128)S(1)}, f32[8,8,2,128]{3,1,2,0:T(8,128)S(1)}, u32[]{:S(2)}, u32[]{:S(2)}) collective-permute-start(f32[8,8,2,128]{3,1,2,0:T(8,128)S(1)} %collective-permute-done.6), channel_id=1, source_target_pairs={{1,0},{2,1},{3,2},{4,3},{5,4},{6,5},{7,6},{0,7},{9,8},{10,9},{11,1... | collective-permute-start | bytes 196616 | tf_op jit(solution)/shard_map/ppermute | solution.py:27
  75.3 1.8 %collective-permute-done.7 = f32[8,8,2,128]{3,1,2,0:T(8,128)S(1)} collective-permute-done((f32[8,8,2,128]{3,1,2,0:T(8,128)S(1)}, f32[8,8,2,128]{3,1,2,0:T(8,128)S(1)}, u32[]{:S(2)}, u32[]{:S(2)}) %collective-permute-start.7) | collective-permute-done | bytes 65568 | tf_op jit(solution)/shard_map/ppermute | solution.py:27
  79.7 0.9 multiply_bitcast_fusion.2
  80.7 0.7 constant_dynamic-update-slice_fusion.24
  81.6 1.0 constant_dynamic-update-slice_fusion.16
  82.6 1.0 copy-done.16
  83.6 1.4 %fusion.23 = (f32[8,8,36,2]{3,1,2,0:T(8,128)}, f32[8,8,36,2]{3,1,2,0:T(8,128)S(1)}) fusion(f32[8,8,36,128]{3,1,2,0:T(8,128)S(1)} %get-tuple-element.87), kind=kLoop, calls=%fused_computation.222 | loop fusion | bytes 73728 | tf_op jit(solution)/shard_map/slice | solution.py:39
  85.0 1.8 %copy.208 = f32[8,8,36,2]{2,1,3,0:T(8,128)S(1)} copy(f32[8,8,36,2]{3,1,2,0:T(8,128)} %get-tuple-element.52) | data formatting | bytes 36864 | tf_op jit(solution)/shard_map/slice | solution.py:39
  86.9 1.2 %copy.210 = f32[8,8,36,2]{2,1,3,0:T(8,128)} copy(f32[8,8,36,2]{3,1,2,0:T(8,128)S(1)} %get-tuple-element.53) | data formatting | bytes 36864 | tf_op jit(solution)/shard_map/slice | solution.py:40
  88.0 3.6 %collective-permute-start.10 = (f32[8,8,36,2]{2,1,3,0:T(8,128)}, f32[8,8,36,2]{2,1,3,0:T(8,128)}, u32[]{:S(2)}, u32[]{:S(2)}) collective-permute-start(f32[8,8,36,2]{2,1,3,0:T(8,128)} %copy.210), channel_id=1, source_target_pairs={{1,0},{2,1},{3,2},{4,3},{5,4},{6,5},{7,6},{0,7},{9,8},{10,9},{11,1... | collective-permute-start | bytes 55304 | tf_op jit(solution)/shard_map/ppermute | solution.py:42
  91.6 0.7 constant_dynamic-update-slice_fusion.23
  92.4 0.8 constant_dynamic-update-slice_fusion.22
  93.1 0.8 constant_dynamic-update-slice_fusion.21
  93.9 0.7 constant_dynamic-update-slice_fusion.29
  94.7 1.1 copy-done.15
  96.1 1.2 %multiply_subtract_fusion.2 = f32[8,8,33,128]{3,1,2,0:T(8,128)} fusion(f32[8,8,33,128]{3,1,2,0:T(8,128)S(1)} %get-tuple-element.93, f32[8,8,33,128]{3,1,2,0:T(8,128)S(1)} %get-tuple-element.92, f32[8,8,33,128]{3,1,2,0:T(8,128)S(1)} %get-tuple-element.60, f32[8,8,33,128]{3,1,2,0:T(8,128)S(1)} %copy-done.19, f32[8,33,128]{2,0,1:T(8,128)S(1)} %get-tuple-element.5), kind=kLoop, calls=%fused_computation.30 | loop fusion | flops 1351680 | bytes 5541888 | tf_op jit(solution)/shard_map/sub | solution.py:96
  97.3 1.5 %copy.209 = f32[8,8,36,2]{3,1,2,0:T(8,128)S(1)} copy(f32[8,8,36,2]{2,1,3,0:T(8,128)} %collective-permute-done.9) | data formatting | bytes 36864 | tf_op jit(solution)/shard_map/ppermute | solution.py:41
  98.9 1.4 %copy.212 = f32[8,8,36,2]{3,1,2,0:T(8,128)S(1)} copy(f32[8,8,36,2]{2,1,3,0:T(8,128)} %collective-permute-done.10) | data formatting | bytes 36864 | tf_op jit(solution)/shard_map/ppermute | solution.py:42
  100.3 1.0 pad_maximum_fusion
  101.9 1.4 %minimum_multiply_fusion.1 = f32[8,8,32,130]{3,1,2,0:T(8,128)S(1)} fusion(f32[8,8,32,131]{3,1,2,0:T(8,128)S(1)} %slice_subtract_fusion), kind=kLoop, calls=%fused_computation.17 | loop fusion | flops 2129920 | bytes 3194880 | tf_op jit(solution)/shard_map/mul | solution.py:85
  103.3 1.5 %fusion.3 = (f32[8,8,32,129]{3,1,2,0:T(8,128)S(1)}, f32[8,8,32,129]{3,1,2,0:T(8,128)S(1)}) fusion(f32[8,8,32,130]{3,1,2,0:T(8,128)S(1)} %minimum_multiply_fusion.1, f32[8,8,36,128]{3,1,2,0:T(8,128)S(1)} %copy-done.3, f32[8,8,36,2]{3,1,2,0:T(8,128)S(1)} %copy.209, f32[8,8,36,2]{3,1,2,0:T(8,128)S(1)} %copy.212), kind=kLoop, calls=%fused_computation.10 | loop fusion | flops 1585152 | bytes 5443584 | tf_op jit(solution)/shard_map/add | solution.py:108
  105.0 0.7 multiply_bitcast_fusion.1
  107.9 0.6 copy-done.6
  108.5 0.7 copy-done.7
  109.4 4.8 %fusion.12 = f32[8,8,32,128]{3,1,2,0:T(8,128)S(1)} fusion(f32[8,9,32,128]{3,1,2,0:T(8,128)S(1)} %copy-done.7, f32[8,8,32,129]{3,1,2,0:T(8,128)S(1)} %multiply_subtract_fusion.1, f32[8,8,33,128]{3,1,2,0:T(8,128)S(1)} %copy-done.6, f32[8,8,32,128]{3,2,1,0:T(8,128)S(1)} %copy-done.20, f32[8,8,32,128]{3,2,1,0:T(8,128)} %slice_dynamic-update-slice_fusion.6, ...), kind=kLoop, calls=%fused_computation.38 | loop fusion | flops 2883584 | bytes 10485760 | tf_op jit(solution)/shard_map/add | solution.py:138
  114.3 1.2 %copy.221 = f32[8,8,32,128]{3,2,1,0:T(8,128)} copy(f32[8,8,32,128]{3,1,2,0:T(8,128)S(1)} %fusion.12) | data formatting | bytes 2097152 | tf_op jit(solution)/shard_map/add | solution.py:138
  (125 shorter events, 8.8 us)
Async XLA Ops:
  0.0 8.2 %copy-start.1 = (f32[8,8,32,128]{3,2,1,0:T(8,128)S(1)}, f32[8,8,32,128]{3,2,1,0:T(8,128)}, u32[]{:S(2)}) copy-start(f32[8,8,32,128]{3,2,1,0:T(8,128)} %param.5) | copy-start | bytes 3145732
  1.9 1.0 copy-start.4
  3.6 39.4 %collective-permute-start = (f32[8,8,2,128]{3,1,2,0:T(8,128)}, f32[8,8,2,128]{3,1,2,0:T(8,128)S(1)}, u32[]{:S(2)}, u32[]{:S(2)}) collective-permute-start(f32[8,8,2,128]{3,1,2,0:T(8,128)} %get-tuple-element.79), channel_id=1, source_target_pairs={{0,8},{8,16},{16,24},{24,0},{1,9},{9,17},{17,25},{25,1},{2,10},{10... | collective-permute-start | bytes 196616 | tf_op jit(solution)/shard_map/ppermute | solution.py:41
  6.5 47.6 %collective-permute-start.8 = (f32[8,8,2,128]{3,1,2,0:T(8,128)}, f32[8,8,2,128]{3,1,2,0:T(8,128)S(1)}, u32[]{:S(2)}, u32[]{:S(2)}) collective-permute-start(f32[8,8,2,128]{3,1,2,0:T(8,128)} %get-tuple-element.78), channel_id=1, source_target_pairs={{8,0},{16,8},{24,16},{0,24},{9,1},{17,9},{25,17},{1,25},{10,2},{18... | collective-permute-start | bytes 196616 | tf_op jit(solution)/shard_map/ppermute | solution.py:42
  14.5 1.5 %copy-start.8 = (f32[8,9,32,128]{3,2,1,0:T(8,128)S(1)}, f32[8,9,32,128]{3,2,1,0:T(8,128)}, u32[]{:S(2)}) copy-start(f32[8,9,32,128]{3,2,1,0:T(8,128)} %get-tuple-element.80) | copy-start | bytes 3538948
  14.5 1.6 %copy-start.9 = (f32[8,9,32,128]{3,2,1,0:T(8,128)S(1)}, f32[8,9,32,128]{3,2,1,0:T(8,128)}, u32[]{:S(2)}) copy-start(f32[8,9,32,128]{3,2,1,0:T(8,128)} %get-tuple-element.81) | copy-start | bytes 3538948
  18.3 8.6 %copy-start = (f32[8,9,32,128]{3,1,2,0:T(8,128)}, f32[8,9,32,128]{3,1,2,0:T(8,128)S(1)}, u32[]{:S(2)}) copy-start(f32[8,9,32,128]{3,1,2,0:T(8,128)S(1)} %get-tuple-element.48) | copy-start | bytes 3538948
  21.2 3.3 %copy-start.10 = (f32[8,9,32,128]{3,1,2,0:T(8,128)}, f32[8,9,32,128]{3,1,2,0:T(8,128)S(1)}, u32[]{:S(2)}) copy-start(f32[8,9,32,128]{3,1,2,0:T(8,128)S(1)} %get-tuple-element.43) | copy-start | bytes 3538948
  25.4 5.2 %copy-start.12 = (f32[8,9,32,128]{3,1,2,0:T(8,128)}, f32[8,9,32,128]{3,1,2,0:T(8,128)S(1)}, u32[]{:S(2)}) copy-start(f32[8,9,32,128]{3,1,2,0:T(8,128)S(1)} %get-tuple-element.45) | copy-start | bytes 3538948
  32.8 5.4 %copy-start.11 = (f32[8,9,32,128]{3,1,2,0:T(8,128)S(1)}, f32[8,9,32,128]{3,1,2,0:T(8,128)}, u32[]{:S(2)}) copy-start(f32[8,9,32,128]{3,1,2,0:T(8,128)} %copy-done.10) | copy-start | bytes 3538948
  32.8 5.4 %copy-start.13 = (f32[8,9,32,128]{3,1,2,0:T(8,128)S(1)}, f32[8,9,32,128]{3,1,2,0:T(8,128)}, u32[]{:S(2)}) copy-start(f32[8,9,32,128]{3,1,2,0:T(8,128)} %copy-done.12) | copy-start | bytes 3538948
  42.9 5.5 %collective-permute-start.1 = (f32[8,8,2,128]{3,1,2,0:T(8,128)S(1)}, f32[8,8,2,128]{3,1,2,0:T(8,128)S(1)}, u32[]{:S(2)}, u32[]{:S(2)}) collective-permute-start(f32[8,8,2,128]{3,1,2,0:T(8,128)S(1)} %collective-permute-done), channel_id=1, source_target_pairs={{0,1},{1,2},{2,3},{3,4},{4,5},{5,6},{6,7},{7,0},{8,9},{9,10},{10,1... | collective-permute-start | bytes 196616 | tf_op jit(solution)/shard_map/ppermute | solution.py:25
  48.4 5.6 %collective-permute-start.2 = (f32[8,8,2,128]{3,1,2,0:T(8,128)S(1)}, f32[8,8,2,128]{3,1,2,0:T(8,128)S(1)}, u32[]{:S(2)}, u32[]{:S(2)}) collective-permute-start(f32[8,8,2,128]{3,1,2,0:T(8,128)S(1)} %collective-permute-done.1), channel_id=1, source_target_pairs={{0,1},{1,2},{2,3},{3,4},{4,5},{5,6},{6,7},{7,0},{8,9},{9,10},{10,1... | collective-permute-start | bytes 196616 | tf_op jit(solution)/shard_map/ppermute | solution.py:25
  48.4 20.6 %collective-permute-start.5 = (f32[8,8,2,128]{3,1,2,0:T(8,128)S(1)}, f32[8,8,2,128]{3,1,2,0:T(8,128)S(1)}, u32[]{:S(2)}, u32[]{:S(2)}) collective-permute-start(f32[8,8,2,128]{3,1,2,0:T(8,128)S(1)} %collective-permute-done), channel_id=1, source_target_pairs={{1,0},{2,1},{3,2},{4,3},{5,4},{6,5},{7,6},{0,7},{9,8},{10,9},{11,1... | collective-permute-start | bytes 196616 | tf_op jit(solution)/shard_map/ppermute | solution.py:27
  54.0 15.6 %collective-permute-start.3 = (f32[8,8,2,128]{3,1,2,0:T(8,128)S(1)}, f32[8,8,2,128]{3,1,2,0:T(8,128)S(1)}, u32[]{:S(2)}, u32[]{:S(2)}) collective-permute-start(f32[8,8,2,128]{3,1,2,0:T(8,128)S(1)} %collective-permute-done.2), channel_id=1, source_target_pairs={{0,1},{1,2},{2,3},{3,4},{4,5},{5,6},{6,7},{7,0},{8,9},{9,10},{10,1... | collective-permute-start | bytes 196616 | tf_op jit(solution)/shard_map/ppermute | solution.py:25
  69.1 2.5 %collective-permute-start.6 = (f32[8,8,2,128]{3,1,2,0:T(8,128)S(1)}, f32[8,8,2,128]{3,1,2,0:T(8,128)S(1)}, u32[]{:S(2)}, u32[]{:S(2)}) collective-permute-start(f32[8,8,2,128]{3,1,2,0:T(8,128)S(1)} %collective-permute-done.5), channel_id=1, source_target_pairs={{1,0},{2,1},{3,2},{4,3},{5,4},{6,5},{7,6},{0,7},{9,8},{10,9},{11,1... | collective-permute-start | bytes 196616 | tf_op jit(solution)/shard_map/ppermute | solution.py:27
  69.7 5.5 %collective-permute-start.4 = (f32[8,8,2,128]{3,1,2,0:T(8,128)S(1)}, f32[8,8,2,128]{3,1,2,0:T(8,128)S(1)}, u32[]{:S(2)}, u32[]{:S(2)}) collective-permute-start(f32[8,8,2,128]{3,1,2,0:T(8,128)S(1)} %collective-permute-done.3), channel_id=1, source_target_pairs={{0,1},{1,2},{2,3},{3,4},{4,5},{5,6},{6,7},{7,0},{8,9},{9,10},{10,1... | collective-permute-start | bytes 196616 | tf_op jit(solution)/shard_map/ppermute | solution.py:25
  71.6 5.5 %collective-permute-start.7 = (f32[8,8,2,128]{3,1,2,0:T(8,128)S(1)}, f32[8,8,2,128]{3,1,2,0:T(8,128)S(1)}, u32[]{:S(2)}, u32[]{:S(2)}) collective-permute-start(f32[8,8,2,128]{3,1,2,0:T(8,128)S(1)} %collective-permute-done.6), channel_id=1, source_target_pairs={{1,0},{2,1},{3,2},{4,3},{5,4},{6,5},{7,6},{0,7},{9,8},{10,9},{11,1... | collective-permute-start | bytes 196616 | tf_op jit(solution)/shard_map/ppermute | solution.py:27
  77.7 1.2 %copy-start.5 = (f32[8,8,32,128]{3,1,2,0:T(8,128)S(1)}, f32[8,8,32,128]{3,1,2,0:T(8,128)}, u32[]{:S(2)}) copy-start(f32[8,8,32,128]{3,1,2,0:T(8,128)} %copy-done.4) | copy-start | bytes 3145732
  78.7 4.9 %copy-start.2 = (f32[8,8,36,128]{3,1,2,0:T(8,128)}, f32[8,8,36,128]{3,1,2,0:T(8,128)S(1)}, u32[]{:S(2)}) copy-start(f32[8,8,36,128]{3,1,2,0:T(8,128)S(1)} %get-tuple-element.87) | copy-start | bytes 3538948
  81.5 1.1 copy-start.18
  82.6 1.0 copy-start.16
  86.8 10.5 %collective-permute-start.9 = (f32[8,8,36,2]{2,1,3,0:T(8,128)S(1)}, f32[8,8,36,2]{2,1,3,0:T(8,128)}, u32[]{:S(2)}, u32[]{:S(2)}) collective-permute-start(f32[8,8,36,2]{2,1,3,0:T(8,128)S(1)} %copy.208), channel_id=1, source_target_pairs={{0,1},{1,2},{2,3},{3,4},{4,5},{5,6},{6,7},{7,0},{8,9},{9,10},{10,1... | collective-permute-start | bytes 55304 | tf_op jit(solution)/shard_map/ppermute | solution.py:41
  88.0 5.9 %copy-start.22 = (f32[1,8,33,128]{3,1,2,0:T(8,128)S(1)}, f32[1,8,33,128]{3,1,2,0:T(8,128)}, u32[]{:S(2)}) copy-start(f32[1,8,33,128]{3,1,2,0:T(8,128)} %get-tuple-element.9) | copy-start | bytes 405508
  88.0 6.5 %copy-start.14 = (f32[8,8,33,128]{3,1,2,0:T(8,128)S(1)}, f32[8,8,33,128]{3,1,2,0:T(8,128)}, u32[]{:S(2)}) copy-start(f32[8,8,33,128]{3,1,2,0:T(8,128)} %get-tuple-element.66) | copy-start | bytes 3244036
  88.0 6.5 %copy-start.17 = (f32[8,8,33,128]{3,1,2,0:T(8,128)S(1)}, f32[8,8,33,128]{3,1,2,0:T(8,128)}, u32[]{:S(2)}) copy-start(f32[8,8,33,128]{3,1,2,0:T(8,128)} %copy-done.16) | copy-start | bytes 3244036
  88.0 10.8 %collective-permute-start.10 = (f32[8,8,36,2]{2,1,3,0:T(8,128)}, f32[8,8,36,2]{2,1,3,0:T(8,128)}, u32[]{:S(2)}, u32[]{:S(2)}) collective-permute-start(f32[8,8,36,2]{2,1,3,0:T(8,128)} %copy.210), channel_id=1, source_target_pairs={{1,0},{2,1},{3,2},{4,3},{5,4},{6,5},{7,6},{0,7},{9,8},{10,9},{11,1... | collective-permute-start | bytes 55304 | tf_op jit(solution)/shard_map/ppermute | solution.py:42
  93.1 1.6 %copy-start.21 = (f32[1,8,33,128]{3,1,2,0:T(8,128)S(1)}, f32[1,8,33,128]{3,1,2,0:T(8,128)}, u32[]{:S(2)}) copy-start(f32[1,8,33,128]{3,1,2,0:T(8,128)} %get-tuple-element.11) | copy-start | bytes 405508
  94.6 1.2 %copy-start.15 = (f32[8,8,33,128]{3,1,2,0:T(8,128)S(1)}, f32[8,8,33,128]{3,1,2,0:T(8,128)}, u32[]{:S(2)}) copy-start(f32[8,8,33,128]{3,1,2,0:T(8,128)} %constant_dynamic-update-slice_fusion.29) | copy-start | bytes 3244036
  94.6 1.6 %copy-start.19 = (f32[8,8,33,128]{3,1,2,0:T(8,128)S(1)}, f32[8,8,33,128]{3,1,2,0:T(8,128)}, u32[]{:S(2)}) copy-start(f32[8,8,33,128]{3,1,2,0:T(8,128)} %get-tuple-element.54) | copy-start | bytes 3244036
  97.3 2.9 %copy-start.3 = (f32[8,8,36,128]{3,1,2,0:T(8,128)S(1)}, f32[8,8,36,128]{3,1,2,0:T(8,128)}, u32[]{:S(2)}) copy-start(f32[8,8,36,128]{3,1,2,0:T(8,128)} %copy-done.2) | copy-start | bytes 3538948
  107.3 1.2 %copy-start.6 = (f32[8,8,33,128]{3,1,2,0:T(8,128)S(1)}, f32[8,8,33,128]{3,1,2,0:T(8,128)}, u32[]{:S(2)}) copy-start(f32[8,8,33,128]{3,1,2,0:T(8,128)} %multiply_subtract_fusion.2) | copy-start | bytes 3244036
  107.3 1.9 %copy-start.7 = (f32[8,9,32,128]{3,1,2,0:T(8,128)S(1)}, f32[8,9,32,128]{3,1,2,0:T(8,128)}, u32[]{:S(2)}) copy-start(f32[8,9,32,128]{3,1,2,0:T(8,128)} %multiply_subtract_fusion) | copy-start | bytes 3538948
  107.3 2.2 %copy-start.20 = (f32[8,8,32,128]{3,2,1,0:T(8,128)S(1)}, f32[8,8,32,128]{3,2,1,0:T(8,128)}, u32[]{:S(2)}) copy-start(f32[8,8,32,128]{3,2,1,0:T(8,128)} %param.4) | copy-start | bytes 3145732
